TPU v7x, 256 devices: a whole 4x4x8 slice. The times are simulated.
256 devices in a mesh: row: 32 (over x, z), col: 8 (over y, core).
Axes of the slice: x: 4, y: 4, z: 8, core: 2. Of those that a mesh axis runs over, the one named last changes fastest.
Arguments:
- incident: float32 [2, 36, 32768], P(None, None, 'row'), may hold values from -24 to 24
- diagonal: float32 [32768], P('row'), may hold values from 1 to 2
- near_blocks: bfloat16 [32, 8, 2, 1024, 1024], P('row', None, None, None, 'col'), may hold values from -0.046875 to 0.046875
- left_factors: bfloat16 [32, 32, 2, 64, 1024], P('row', 'col'), may hold values from -0.0390625 to 0.0390625
- right_factors: bfloat16 [32, 32, 2, 64, 1024], P('row', 'col'), may hold values from -0.1875 to 0.1875
- flags: int32 [32, 8], P('row'), may hold values from 0 to 1, as said below
- ranks: int32 [32, 32], P('row', 'col'), may hold values from 4 to 64
- harmonics: float32 [2, 36, 32768], P(None, None, 'row'), may hold values from -0.03125 to 0.03125
Outputs:
- solution: float32 [2, 36, 32768], P(None, None, 'row')
- coefficients: float32 [2, 36, 36], replicated
Inputs may be any that keep to these rules, and one draw needn't show every extreme that they name: `flags`: slot 8 / 2 (the pair of a cluster with itself) is always 1; the ones of a row form one run of slots around it.
All inputs are finite; a program needn't handle non-finite values.
Results may differ from a plain program's by a relative error of at most 0.0013.
Values may be sent and summed in bfloat16 or wider, within the bound.
A program may use at most 128 MiB of HBM per device.

v0:
```python
from functools import partial
import jax
import jax.numpy as jnp
from jax import lax
from jax.sharding import PartitionSpec as P

highest = lax.Precision.HIGHEST


def dense_term(vector, block):

    def product(left, right):
        return jnp.einsum("sf,ef->se", left, right, preferred_element_type=jnp.float32)

    real_out = product(vector[0], block[0]) - product(vector[1], block[1])
    imag_out = product(vector[0], block[1]) + product(vector[1], block[0])
    return jnp.stack([real_out, imag_out])


def lowrank_term(vector, left_block, right_block, rank):

    def inner(left, right):
        return jnp.einsum("sf,rf->sr", left, right, preferred_element_type=jnp.float32)

    def outer(left, right):
        return jnp.einsum("sr,re->se", left, right, preferred_element_type=jnp.float32)

    coeff_real = inner(vector[0], right_block[0]) - inner(vector[1], right_block[1])
    coeff_imag = inner(vector[0], right_block[1]) + inner(vector[1], right_block[0])
    keep = (jnp.arange(right_block.shape[1], dtype=jnp.int32) < rank)[None, None, :]
    coeffs = jnp.where(keep, jnp.stack([coeff_real, coeff_imag]), 0.0).astype(jnp.bfloat16)
    real_out = outer(coeffs[0], left_block[0]) - outer(coeffs[1], left_block[1])
    imag_out = outer(coeffs[0], left_block[1]) + outer(coeffs[1], left_block[0])
    return jnp.stack([real_out, imag_out])


def inner_products(first, second):
    return jnp.einsum("csn,ctn->st", first, second, precision=highest)


def combine_rows(matrix, vectors):
    return jnp.einsum("st,ctn->csn", matrix, vectors, precision=highest)


def matmul(left, right):
    return jnp.dot(left, right, precision=highest)


def lower_inverse(lower):
    identity = jnp.eye(lower.shape[0], dtype=lower.dtype)
    return lax.linalg.triangular_solve(lower, identity, left_side=True, lower=True)


def project(harmonics, vectors):

    def contract(left, right):
        return jnp.einsum("mn,sn->ms", left, right, precision=highest)

    real_out = contract(harmonics[0], vectors[0]) + contract(harmonics[1], vectors[1])
    imag_out = contract(harmonics[0], vectors[1]) - contract(harmonics[1], vectors[0])
    return jnp.stack([real_out, imag_out])


def body(incident, diagonal, near_blocks, left_factors, right_factors, flags, ranks, harmonics):
    blocks = left_factors.shape[1]
    slots = near_blocks.shape[1]
    width = near_blocks.shape[4]
    half_band = slots // 2
    elements = incident.shape[2]
    fields = incident.shape[1]
    clusters = lax.axis_size("row")
    row_index = lax.axis_index("row")
    column = lax.axis_index("col")
    empty = jnp.zeros((2, fields, elements), jnp.float32)

    def far_term(number, piece):
        cluster = column * blocks + number
        offset = (cluster - row_index + half_band) % clusters
        is_near = (offset < slots) & (flags[0, jnp.minimum(offset, slots - 1)] == 1)
        return lax.cond(
            is_near,
            lambda operand: empty,
            partial(
                lowrank_term,
                left_block=left_factors[0, number],
                right_block=right_factors[0, number],
                rank=ranks[0, number],
            ),
            piece,
        )

    def near_term(slot, piece):
        return lax.cond(
            flags[0, slot] == 1,
            partial(dense_term, block=near_blocks[0, slot]),
            lambda operand: empty,
            piece,
        )

    def apply_operator(vector):
        rounded = vector.astype(jnp.bfloat16)
        gathered = lax.all_gather(rounded, "row", axis=2, tiled=True)
        far_pieces = [
            lax.dynamic_slice_in_dim(gathered, (column * blocks + number) * elements, elements, 2)
            for number in range(blocks)
        ]
        near_pieces = [
            lax.dynamic_slice_in_dim(
                gathered,
                (row_index + slot - half_band) % clusters * elements + column * width,
                width,
                2,
            )
            for slot in range(slots)
        ]
        total = near_term(0, near_pieces[0])
        for slot in range(1, slots):
            total = total + near_term(slot, near_pieces[slot])
        for number in range(blocks):
            total = total + far_term(number, far_pieces[number])
        summed = lax.psum(total, "col")
        return summed + diagonal[None, None, :] * vector

    lower_first = jnp.linalg.cholesky(lax.psum(inner_products(incident, incident), "row"))
    basis_one = combine_rows(lower_inverse(lower_first), incident)
    image = apply_operator(basis_one)
    coupling_one = lax.psum(inner_products(image, basis_one), "row")
    rest = image - combine_rows(coupling_one, basis_one)
    gram_one = lax.psum(inner_products(rest, rest), "row")
    lower_second = jnp.linalg.cholesky(gram_one)
    basis_two = combine_rows(lower_inverse(lower_second), rest)
    image = apply_operator(basis_two)
    coupling_onetwo, coupling_two = lax.psum(
        (inner_products(image, basis_one), inner_products(image, basis_two)), "row"
    )
    rest = image - combine_rows(coupling_onetwo, basis_one) - combine_rows(coupling_two, basis_two)
    gram_two = lax.psum(inner_products(rest, rest), "row")
    upper_left = matmul(coupling_one, coupling_one.T) + gram_one
    upper_right = matmul(coupling_one, coupling_onetwo.T) + matmul(lower_second, coupling_two.T)
    lower_right = (
        matmul(coupling_onetwo, coupling_onetwo.T) + matmul(coupling_two, coupling_two.T) + gram_two
    )
    normal = jnp.concatenate(
        [
            jnp.concatenate([upper_left, upper_right], axis=1),
            jnp.concatenate([upper_right.T, lower_right], axis=1),
        ],
        axis=0,
    )
    target = jnp.concatenate(
        [matmul(lower_first, coupling_one.T), matmul(lower_first, coupling_onetwo.T)], axis=1
    )
    factor_inverse = lower_inverse(jnp.linalg.cholesky(normal))
    weights = matmul(factor_inverse.T, matmul(factor_inverse, target.T)).T
    first_weights = weights[:, :fields]
    second_weights = weights[:, fields:]
    solution = combine_rows(first_weights, basis_one) + combine_rows(second_weights, basis_two)
    coefficients = lax.psum(project(harmonics, solution), "row")
    return (solution, coefficients)


def solution(mesh):
    in_specs = (
        P(None, None, "row"),
        P("row"),
        P("row", None, None, None, "col"),
        P("row", "col", None, None, None),
        P("row", "col", None, None, None),
        P("row", None),
        P("row", "col"),
        P(None, None, "row"),
    )
    out_specs = (P(None, None, "row"), P())
    return jax.shard_map(body, mesh=mesh, in_specs=in_specs, out_specs=out_specs, check_vma=False)
```

profile of v0, /device:TPU:0, one launch (start us, length us, event | category | flops | bytes accessed | tf_op | source)
XLA Modules:
  0.0 1355.9 jit_solution(15684794761179191939)
XLA Ops:
  8.8 144.0 %psum.63 = f32[36,36]{0,1:T(8,128)S(1)} all-reduce(f32[36,36]{0,1:T(8,128)S(1)} %convolution_bitcast_fusion.12), channel_id=1, replica_groups=mesh['row'=32,'col'=8] {'row'}, use_global_device_ids=true, to_apply=%region_0.0 | all-reduce | flops 1296 | bytes 10368 | tf_op jit(solution)/shard_map/psum | solution.py:124
  178.0 64.0 %all-gather.3.cloned.1.call-done = bf16[2,36,32768]{2,1,0:T(8,128)(2,1)} async-done(((bf16[2,36,1024]{2,1,0:T(8,128)(2,1)}), bf16[2,36,32768]{2,1,0:T(8,128)(2,1)}) %all-gather.3.cloned.1.call-update) | async-done | bytes 4718608 | tf_op jit(solution)/shard_map/all_gather | solution.py:102
  245.0 6.4 conditional.31
  251.5 6.4 conditional.30
  257.9 4.9 conditional.29
  262.8 4.9 conditional.28
  267.7 4.8 conditional.27
  272.5 4.8 conditional.26
  277.3 4.8 conditional.24
  282.1 4.8 conditional.25
  290.0 99.7 %all-reduce.4.cloned.1.call-done = f32[2,36,1024]{2,1,0:T(8,128)} async-done(((f32[2,36,1024]{2,1,0:T(8,128)}), f32[2,36,1024]{2,1,0:T(8,128)}) %all-reduce.4.cloned.1.call-update) | async-done | bytes 294928 | tf_op jit(solution)/shard_map/psum | solution.py:121
  391.1 143.1 %psum.65 = f32[36,36]{1,0:T(8,128)S(1)} all-reduce(f32[36,36]{1,0:T(8,128)S(1)} %convolution_bitcast_fusion.10), channel_id=1, replica_groups=mesh['row'=32,'col'=8] {'row'}, use_global_device_ids=true, to_apply=%region_28.31 | all-reduce | flops 1296 | bytes 10368 | tf_op jit(solution)/shard_map/psum | solution.py:127
  536.7 137.9 %psum.66 = f32[36,36]{1,0:T(8,128)S(1)} all-reduce(f32[36,36]{1,0:T(8,128)S(1)} %convolution_bitcast_fusion.9), channel_id=1, replica_groups=mesh['row'=32,'col'=8] {'row'}, use_global_device_ids=true, to_apply=%region_29.32 | all-reduce | flops 1296 | bytes 10368 | tf_op jit(solution)/shard_map/psum | solution.py:129
  687.5 73.5 %all-gather.5.cloned.1.call-done = bf16[2,36,32768]{2,1,0:T(8,128)(2,1)} async-done(((bf16[2,36,1024]{2,1,0:T(8,128)(2,1)}), bf16[2,36,32768]{2,1,0:T(8,128)(2,1)}) %all-gather.5.cloned.1.call-update) | async-done | bytes 4718608 | tf_op jit(solution)/shard_map/all_gather | solution.py:102
  764.1 5.7 conditional.43
  769.9 5.7 conditional.42
  775.6 5.7 conditional.41
  790.8 4.9 conditional.38
  807.4 97.7 %all-reduce.6.cloned.1.call-done = f32[2,36,1024]{2,1,0:T(8,128)} async-done(((f32[2,36,1024]{2,1,0:T(8,128)}), f32[2,36,1024]{2,1,0:T(8,128)}) %all-reduce.6.cloned.1.call-update) | async-done | bytes 294928 | tf_op jit(solution)/shard_map/psum | solution.py:121
  907.8 143.1 %all-reduce = (f32[36,36]{1,0:T(8,128)S(1)}, f32[36,36]{1,0:T(8,128)S(1)}) all-reduce(f32[36,36]{1,0:T(8,128)S(1)} %convolution_bitcast_fusion.7, f32[36,36]{1,0:T(8,128)S(1)} %convolution_bitcast_fusion.6), channel_id=1, replica_groups=mesh['row'=32,'col'=8] {'row'}, use_global_device_ids=true, to_apply=%region_55.58 | all-reduce | flops 2592 | bytes 20736 | tf_op jit(solution)/shard_map/psum | solution.py:133
  1054.4 137.9 %psum.70 = f32[36,36]{0,1:T(8,128)S(1)} all-reduce(f32[36,36]{0,1:T(8,128)S(1)} %convolution_bitcast_fusion.5), channel_id=1, replica_groups=mesh['row'=32,'col'=8] {'row'}, use_global_device_ids=true, to_apply=%region_57.60 | all-reduce | flops 1296 | bytes 10368 | tf_op jit(solution)/shard_map/psum | solution.py:137
  1193.7 6.6 cholesky.42
  1201.6 5.5 custom-call.11
  1210.9 137.7 %psum.71 = f32[2,36,36]{1,2,0:T(8,128)S(1)} all-reduce(f32[2,36,36]{1,2,0:T(8,128)S(1)} %pad_maximum_fusion.24), channel_id=1, replica_groups=mesh['row'=32,'col'=8] {'row'}, use_global_device_ids=true, to_apply=%region_60.63 | all-reduce | flops 2592 | bytes 20736 | tf_op jit(solution)/shard_map/psum | solution.py:158
  (212 shorter events, 166.1 us)
Async XLA Ops:
  7.2 234.8 %all-gather.3.cloned.1.call-start = ((), (), s32[]{:S(2)}) async-start(), calls=%async_computation | async-start | bytes 5406720 | tf_op jit(solution)/shard_map/all_gather | solution.py:102
  156.2 4.1 copy-start.15
  162.7 227.0 %all-reduce.4.cloned.1.call-start = ((), (), s32[]{:S(2)}) async-start(), calls=%async_computation.1 | async-start | bytes 655360 | tf_op jit(solution)/shard_map/psum | solution.py:121
  172.2 4.4 copy-start.3
  178.0 79.9 %copy-start = (bf16[2,1024,128]{2,1,0:T(8,128)(2,1)}, bf16[2,1024,128]{2,1,0:T(8,128)(2,1)S(1)}, u32[]{:S(2)}) copy-start(bf16[2,1024,128]{2,1,0:T(8,128)(2,1)S(1)} %get-tuple-element.571) | copy-start | bytes 1572868
  262.8 4.9 copy-start.10
  272.5 14.4 %copy-start.6 = (f32[2,36,1024]{2,1,0:T(8,128)S(1)}, f32[2,36,1024]{2,1,0:T(8,128)}, u32[]{:S(2)}) copy-start(f32[2,36,1024]{2,1,0:T(8,128)} %get-tuple-element.623) | copy-start | bytes 884740
  277.3 112.4 %copy-start.19 = (f32[1024]{0:T(1024)S(1)}, f32[1024]{0:T(1024)}, u32[]{:S(2)}) copy-start(f32[1024]{0:T(1024)} %param.60) | copy-start | bytes 12292
  290.0 471.1 %all-gather.5.cloned.1.call-start = ((), (), s32[]{:S(2)}) async-start(), calls=%async_computation.2 | async-start | bytes 5406720 | tf_op jit(solution)/shard_map/all_gather | solution.py:102
  534.2 226.9 %copy-start.13 = (f32[36,36]{1,0:T(8,128)}, f32[36,36]{1,0:T(8,128)S(1)}, u32[]{:S(2)}) copy-start(f32[36,36]{1,0:T(8,128)S(1)} %psum.65) | copy-start | bytes 15556
  678.1 4.1 copy-start.17
  684.5 220.5 %all-reduce.6.cloned.1.call-start = ((), (), s32[]{:S(2)}) async-start(), calls=%async_computation.3 | async-start | bytes 655360 | tf_op jit(solution)/shard_map/psum | solution.py:121
  761.1 2.3 copy-start.1
  785.4 0.7 copy-start.11
  790.8 13.1 copy-start.7
  790.8 13.1 copy-start.8
  790.8 13.1 copy-start.9
  795.7 8.2 copy-start.12
  795.7 10.8 copy-start.14
  795.7 10.8 copy-start.16
  803.9 388.4 %copy-start.18 = (f32[36,36]{1,0:T(8,128)S(1)}, f32[36,36]{1,0:T(8,128)}, u32[]{:S(2)}) copy-start(f32[36,36]{1,0:T(8,128)} %copy-done.17) | copy-start | bytes 15556
  803.9 389.2 %copy-start.20 = (f32[36,36]{1,0:T(8,128)S(1)}, f32[36,36]{1,0:T(8,128)}, u32[]{:S(2)}) copy-start(f32[36,36]{1,0:T(8,128)} %convolution_add_fusion.36) | copy-start | bytes 15556
  806.5 403.3 %copy-start.5 = (f32[1,36,1024]{2,0,1:T(1,128)S(1)}, f32[1,36,1024]{2,0,1:T(1,128)}, u32[]{:S(2)}) copy-start(f32[1,36,1024]{2,0,1:T(1,128)} %get-tuple-element.587) | copy-start | bytes 442372
  806.5 403.9 %copy-start.4 = (f32[1,36,1024]{2,0,1:T(1,128)S(1)}, f32[1,36,1024]{2,0,1:T(1,128)}, u32[]{:S(2)}) copy-start(f32[1,36,1024]{2,0,1:T(1,128)} %get-tuple-element.586) | copy-start | bytes 442372
  (1 other events, 0.7 us)
Sparse Core Ops, SparseCore 0:
  162.8 79.1 all-gather.2
  290.1 99.5 all-reduce.3
  684.7 76.3 all-gather.4
  806.6 98.3 all-reduce.5
where the time goes:
time: 1360 us
  blocking collectives  844 us (62%)
  waiting for transfers between devices  335 us (25%)
  matrix products  92.1 us (7%)
  other arithmetic  43.3 us (3%)
  between operations  21.8 us (2%)
  local copies, waits for them, and re-layouts  19.4 us (1%)
    psum x2, waiting for transfers between devices, apply_operator(): summed = lax.psum(total, 'col')  197 us
    psum x1, blocking collectives, body(): lax.psum(inner_products(incident, incident), 'row')  144 us
    psum x1, blocking collectives, body(): lax.psum((inner_products(image, basis_one), inner_products(image, basis_t...  143 us
    psum x1, blocking collectives, body(): coupling_one = lax.psum(inner_products(image, basis_one), 'row')  143 us
    psum x1, blocking collectives, body(): gram_two = lax.psum(inner_products(rest, rest), 'row')  138 us
    psum x1, blocking collectives, body(): gram_one = lax.psum(inner_products(rest, rest), 'row')  138 us
    psum x1, blocking collectives, body(): coefficients = lax.psum(project(harmonics, solution), 'row')  138 us
    all_gather x2, waiting for transfers between devices, apply_operator(): gathered = lax.all_gather(rounded, 'row', axis=2, tiled=True)  138 us
  transfers between devices with their start and end apart: 4, of which 4 were waited for; matrix products, arithmetic and copies ran while one was open for 1% of the time, Pallas kernels for 0%

commit v1 on v0

--- a/solution.py
+++ b/solution.py
@@ -99,7 +99,9 @@
 
     def apply_operator(vector):
         rounded = vector.astype(jnp.bfloat16)
-        gathered = lax.all_gather(rounded, "row", axis=2, tiled=True)
+        gathered = jnp.concatenate(
+            lax.all_to_all(jnp.stack([rounded] * lax.axis_size("row")), "row", 0, 0), axis=2
+        )
         far_pieces = [
             lax.dynamic_slice_in_dim(gathered, (column * blocks + number) * elements, elements, 2)
             for number in range(blocks)

time: 1360 us -> 1560 us (1.15)
  local copies, waits for them, and re-layouts: 19.4 us -> 180 us
    all_gather x2 -> x0, waiting for transfers between devices: 138 us -> none  [apply_operator(): gathered = lax.all_gather(rounded, 'row', axis=2, tiled=True)]
    all_to_all x0 -> x2, waiting for transfers between devices: none -> 117 us  [apply_operator(): lax.all_to_all(jnp.stack([rounded] * lax.axis_size('row')), 'row', 0, 0)]
    another operation x0 -> x18, local copies, waits for them, and re-layouts: none -> 92.3 us
    cond x0 -> x56, local copies, waits for them, and re-layouts: none -> 49.9 us
    psum x2, waiting for transfers between devices: 197 us -> 223 us  [apply_operator(): summed = lax.psum(total, 'col')]
    reshape x0 -> x2, local copies, waits for them, and re-layouts: none -> 19.1 us  [apply_operator(): jnp.concatenate(lax.all_to_all(jnp.stack([rounded] * lax.axis_size('row')...]
  transfers between devices with their start and end apart: 4 -> 4, of which waited for: 4 -> 4; matrix products, arithmetic and copies ran while one was open for 1% -> 0% of each run, Pallas kernels for 0% -> 0%
where the time goes in v1:
time: 1560 us; the launch traced here: 1540 us
  blocking collectives  856 us (55%)
  waiting for transfers between devices  340 us (22%)
  local copies, waits for them, and re-layouts  180 us (12%)
  matrix products  80.6 us (5%)
  other arithmetic  40 us (3%)
  between operations  22.6 us (1%)
    psum x2, waiting for transfers between devices, apply_operator(): summed = lax.psum(total, 'col')  223 us
    psum x1, blocking collectives, body(): lax.psum(inner_products(incident, incident), 'row')  148 us
    psum x1, blocking collectives, body(): gram_one = lax.psum(inner_products(rest, rest), 'row')  147 us
    psum x1, blocking collectives, body(): lax.psum((inner_products(image, basis_one), inner_products(image, basis_t...  143 us
    psum x1, blocking collectives, body(): coupling_one = lax.psum(inner_products(image, basis_one), 'row')  143 us
    psum x1, blocking collectives, body(): coefficients = lax.psum(project(harmonics, solution), 'row')  138 us
    psum x1, blocking collectives, body(): gram_two = lax.psum(inner_products(rest, rest), 'row')  138 us
    all_to_all x2, waiting for transfers between devices, apply_operator(): lax.all_to_all(jnp.stack([rounded] * lax.axis_size('row')), 'row', 0, 0)  117 us
  transfers between devices with their start and end apart: 4, of which 4 were waited for; matrix products, arithmetic and copies ran while one was open for 0% of the time, Pallas kernels for 0%

profile of v1, /device:TPU:0, one launch (start us, length us, event | category | flops | bytes accessed | tf_op | source)
XLA Modules:
  0.0 1543.6 jit_solution(16733102701394399664)
XLA Ops:
  8.8 148.0 %psum.63 = f32[36,36]{0,1:T(8,128)S(1)} all-reduce(f32[36,36]{0,1:T(8,128)S(1)} %convolution_bitcast_fusion.7), channel_id=1, replica_groups=mesh['row'=32,'col'=8] {'row'}, use_global_device_ids=true, to_apply=%region_0.0 | all-reduce | flops 1296 | bytes 10368 | tf_op jit(solution)/shard_map/psum | solution.py:126
  190.7 62.2 %all-to-all-done = bf16[32,2,36,1024]{3,1,2,0:T(2,128)(2,1)} async-done(((bf16[32,2,36,1024]{3,1,2,0:T(2,128)(2,1)}), bf16[32,2,36,1024]{3,1,2,0:T(2,128)(2,1)}, u32[]{:S(2)}, u32[]{:S(2)}) %all-to-all-start) | async-done | bytes 4718624 | tf_op jit(solution)/shard_map/all_to_all | solution.py:103
  262.4 12.6 conditional.31
  275.0 12.4 conditional.30
  287.5 12.5 conditional.29
  300.0 12.6 conditional.27
  312.6 12.4 conditional.26
  325.1 13.1 conditional.24
  338.1 13.5 conditional.25
  351.6 12.4 conditional.28
  376.3 121.2 %all-reduce.4.cloned.1.call-done = f32[2,36,1024]{2,0,1:T(2,128)} async-done(((f32[2,36,1024]{2,0,1:T(2,128)}), f32[2,36,1024]{2,0,1:T(2,128)}) %all-reduce.4.cloned.1.call-update) | async-done | bytes 294928 | tf_op jit(solution)/shard_map/psum | solution.py:123
  499.9 143.1 %psum.65 = f32[36,36]{1,0:T(8,128)S(1)} all-reduce(f32[36,36]{1,0:T(8,128)S(1)} %convolution_bitcast_fusion.5), channel_id=1, replica_groups=mesh['row'=32,'col'=8] {'row'}, use_global_device_ids=true, to_apply=%region_28.31 | all-reduce | flops 1296 | bytes 10368 | tf_op jit(solution)/shard_map/psum | solution.py:129
  646.0 146.8 %psum.66 = f32[36,36]{1,0:T(8,128)S(1)} all-reduce(f32[36,36]{1,0:T(8,128)S(1)} %convolution_bitcast_fusion.4), channel_id=1, replica_groups=mesh['row'=32,'col'=8] {'row'}, use_global_device_ids=true, to_apply=%region_29.32 | all-reduce | flops 1296 | bytes 10368 | tf_op jit(solution)/shard_map/psum | solution.py:131
  818.6 54.5 %all-to-all-done.1 = bf16[32,2,36,1024]{3,1,2,0:T(2,128)(2,1)} async-done(((bf16[32,2,36,1024]{3,1,2,0:T(2,128)(2,1)}), bf16[32,2,36,1024]{3,1,2,0:T(2,128)(2,1)}, u32[]{:S(2)}, u32[]{:S(2)}) %all-to-all-start.1) | async-done | bytes 4718624 | tf_op jit(solution)/shard_map/all_to_all | solution.py:103
  882.6 13.5 conditional.37
  896.1 13.1 conditional.36
  909.2 12.5 conditional.38
  921.6 11.0 conditional.39
  954.5 11.1 conditional.42
  966.6 11.6 conditional.43
  991.1 102.3 %all-reduce.6.cloned.1.call-done = f32[2,36,1024]{2,0,1:T(2,128)} async-done(((f32[2,36,1024]{2,0,1:T(2,128)}), f32[2,36,1024]{2,0,1:T(2,128)}) %all-reduce.6.cloned.1.call-update) | async-done | bytes 294928 | tf_op jit(solution)/shard_map/psum | solution.py:123
  1095.5 143.1 %all-reduce = (f32[36,36]{1,0:T(8,128)S(1)}, f32[36,36]{1,0:T(8,128)S(1)}) all-reduce(f32[36,36]{1,0:T(8,128)S(1)} %convolution_bitcast_fusion.1, f32[36,36]{1,0:T(8,128)S(1)} %convolution_bitcast_fusion.2), channel_id=1, replica_groups=mesh['row'=32,'col'=8] {'row'}, use_global_device_ids=true, to_apply=%region_56.59 | all-reduce | flops 2592 | bytes 20736 | tf_op jit(solution)/shard_map/psum | solution.py:135
  1242.8 137.7 %psum.70 = f32[36,36]{0,1:T(8,128)S(1)} all-reduce(f32[36,36]{0,1:T(8,128)S(1)} %convolution_bitcast_fusion), channel_id=1, replica_groups=mesh['row'=32,'col'=8] {'row'}, use_global_device_ids=true, to_apply=%region_57.60 | all-reduce | flops 1296 | bytes 10368 | tf_op jit(solution)/shard_map/psum | solution.py:139
  1398.2 137.7 %psum.71 = f32[2,36,36]{1,2,0:T(8,128)S(1)} all-reduce(f32[2,36,36]{1,2,0:T(8,128)S(1)} %pad_maximum_fusion.24), channel_id=1, replica_groups=mesh['row'=32,'col'=8] {'row'}, use_global_device_ids=true, to_apply=%region_60.63 | all-reduce | flops 2592 | bytes 20736 | tf_op jit(solution)/shard_map/psum | solution.py:160
  (304 shorter events, 346.0 us)
Async XLA Ops:
  172.8 5.3 copy-start.56
  172.8 13.6 copy-start.58
  172.8 14.3 copy-start.51
  172.8 14.3 copy-start.52
  172.8 80.1 %all-to-all-start = ((bf16[32,2,36,1024]{3,1,2,0:T(2,128)(2,1)}), bf16[32,2,36,1024]{3,1,2,0:T(2,128)(2,1)}, u32[]{:S(2)}, u32[]{:S(2)}) async-start(bf16[32,2,36,1024]{3,1,2,0:T(2,128)(2,1)} %stack.463), calls=%async_computation | async-start | bytes 9437184 | tf_op jit(solution)/shard_map/all_to_all | solution.py:103
  177.8 319.7 %all-reduce.4.cloned.1.call-start = ((), (), s32[]{:S(2)}) async-start(), calls=%async_computation.2 | async-start | bytes 589824 | tf_op jit(solution)/shard_map/psum | solution.py:123
  186.4 2.9 copy-start.41
  267.5 2.4 copy-start.25
  305.1 2.4 copy-start.28
  325.1 7.4 copy-start
  330.1 2.4 copy-start.30
  338.5 7.4 copy-start.2
  365.9 131.6 %copy-start.57 = (f32[1024]{0:T(1024)S(1)}, f32[1024]{0:T(1024)}, u32[]{:S(2)}) copy-start(f32[1024]{0:T(1024)} %param.60) | copy-start | bytes 12292
  796.2 14.6 copy-start.53
  810.9 62.2 %all-to-all-start.1 = ((bf16[32,2,36,1024]{3,1,2,0:T(2,128)(2,1)}), bf16[32,2,36,1024]{3,1,2,0:T(2,128)(2,1)}, u32[]{:S(2)}, u32[]{:S(2)}) async-start(bf16[32,2,36,1024]{3,1,2,0:T(2,128)(2,1)} %stack.464), calls=%async_computation.1 | async-start | bytes 9437184 | tf_op jit(solution)/shard_map/all_to_all | solution.py:103
  815.7 277.6 %all-reduce.6.cloned.1.call-start = ((), (), s32[]{:S(2)}) async-start(), calls=%async_computation.3 | async-start | bytes 589824 | tf_op jit(solution)/shard_map/psum | solution.py:123
  883.0 7.4 copy-start.3
  896.1 7.4 copy-start.1
  982.8 5.0 copy-start.50
  982.8 110.6 %copy-start.4 = (f32[2,36,1024]{2,0,1:T(2,128)S(1)}, f32[2,36,1024]{2,0,1:T(2,128)}, u32[]{:S(2)}) copy-start(f32[2,36,1024]{2,0,1:T(2,128)} %get-tuple-element.863) | copy-start | bytes 884740
  987.8 253.1 %copy-start.54 = (f32[36,36]{1,0:T(8,128)S(1)}, f32[36,36]{1,0:T(8,128)}, u32[]{:S(2)}) copy-start(f32[36,36]{1,0:T(8,128)} %copy-done.53) | copy-start | bytes 15556
  987.8 253.9 %copy-start.55 = (f32[36,36]{1,0:T(8,128)S(1)}, f32[36,36]{1,0:T(8,128)}, u32[]{:S(2)}) copy-start(f32[36,36]{1,0:T(8,128)} %convolution_add_fusion.36) | copy-start | bytes 15556
  987.8 408.3 %copy-start.45 = (f32[1,36,1024]{2,0,1:T(1,128)S(1)}, f32[1,36,1024]{2,0,1:T(1,128)}, u32[]{:S(2)}) copy-start(f32[1,36,1024]{2,0,1:T(1,128)} %get-tuple-element.883) | copy-start | bytes 442372
  990.2 407.4 %copy-start.44 = (f32[1,36,1024]{2,0,1:T(1,128)S(1)}, f32[1,36,1024]{2,0,1:T(1,128)}, u32[]{:S(2)}) copy-start(f32[1,36,1024]{2,0,1:T(1,128)} %get-tuple-element.882) | copy-start | bytes 442372
  (27 other events, 43.1 us)
Sparse Core Ops, SparseCore 0:
  376.4 121.0 all-reduce.3
  990.4 102.9 all-reduce.5
